TPU v7x, 1024 devices: a whole 4x8x16 slice. The times are simulated.
1024 devices in a mesh: dp: 128 (over x, z, core), tensor: 8 (over y).
Axes of the slice: x: 4, y: 8, z: 16, core: 2. Of those that a mesh axis runs over, the one named last changes fastest.
Arguments:
- hidden: bfloat16 [16384, 28672], P('dp', 'tensor'), may hold values from -6 to 6
- out_grad: bfloat16 [16384, 8192], P('dp'), may hold values from -24 to 24
- prev_hidden: bfloat16 [16384, 28672], P('dp', 'tensor'), may hold values from -6 to 6
- prev_grad: bfloat16 [16384, 8192], P('dp'), may hold values from -24 to 24
- prev_basis: float32 [28672, 32], P('tensor'), may hold values from -6 to 6
- warm_start: float32 [8192, 32], replicated, may hold values from -0.17 to 0.17
Outputs:
- new_basis: float32 [28672, 32], P('tensor')
- new_factor: float32 [8192, 32], P('dp')
All inputs are finite; a program needn't handle non-finite values.
Results may differ from a plain program's by a relative error of at most 0.007.
Values sent between devices are 32-bit elements; how exact they have to be, the bound alone decides.
A program may use at most 32 MiB of HBM per device.

v0:
```python
import jax
import jax.numpy as jnp
from jax import lax
from jax.sharding import PartitionSpec as P

FF = 28672


def orthonormal(rows_in, gram_matrix, norm_scale):
    lower = jnp.linalg.cholesky(gram_matrix)
    return norm_scale * jax.scipy.linalg.solve_triangular(lower, rows_in.T, lower=True).T


def on_device(hidden, out_grad, prev_hidden, prev_grad, prev_basis, warm_start):
    highest = lax.Precision.HIGHEST
    replicas = lax.axis_size("dp")
    norm_scale = jnp.sqrt(jnp.float32(FF))
    warm_low = warm_start.astype(jnp.bfloat16)
    projected = jnp.dot(out_grad, warm_low, preferred_element_type=jnp.float32).astype(jnp.bfloat16)
    projected_prev = jnp.dot(prev_grad, warm_low, preferred_element_type=jnp.float32).astype(
        jnp.bfloat16
    )
    coupling = jnp.dot(warm_start.T, warm_start, precision=highest)
    summed = jnp.einsum("tf,tr->fr", hidden, projected, preferred_element_type=jnp.float32)
    summed = summed + jnp.einsum(
        "tf,tr->fr", prev_hidden, projected_prev, preferred_element_type=jnp.float32
    )
    local_p = (summed - jnp.dot(prev_basis, coupling, precision=highest)) / replicas
    p_mean = lax.psum(local_p, "dp")
    gram_matrix = lax.psum(jnp.dot(p_mean.T, p_mean, precision=highest), "tensor")
    new_basis = orthonormal(p_mean, gram_matrix, norm_scale)
    basis_low = new_basis.astype(jnp.bfloat16)
    pulled = jnp.dot(hidden, basis_low, preferred_element_type=jnp.float32).astype(jnp.bfloat16)
    pulled_prev = jnp.dot(prev_hidden, basis_low, preferred_element_type=jnp.float32).astype(
        jnp.bfloat16
    )
    cross_basis = jnp.dot(prev_basis.T, new_basis, precision=highest)
    summed_q = jnp.einsum("td,tr->dr", out_grad, pulled, preferred_element_type=jnp.float32)
    summed_q = summed_q + jnp.einsum(
        "td,tr->dr", prev_grad, pulled_prev, preferred_element_type=jnp.float32
    )
    local_q = (summed_q - jnp.dot(warm_start, cross_basis, precision=highest)) / replicas
    row_count = warm_start.shape[0] // replicas
    summed_all = lax.psum(local_q, ("dp", "tensor"))
    owned_rows = lax.dynamic_slice_in_dim(
        summed_all, lax.axis_index("dp") * row_count, row_count, 0
    )
    return (new_basis, owned_rows / norm_scale)


def solution(mesh):
    return jax.shard_map(
        on_device,
        mesh=mesh,
        in_specs=(
            P("dp", "tensor"),
            P("dp", None),
            P("dp", "tensor"),
            P("dp", None),
            P("tensor", None),
            P(),
        ),
        out_specs=(P("tensor", None), P("dp", None)),
        check_vma=False,
    )
```

profile of v0, /device:TPU:1, one launch (start us, length us, event | category | flops | bytes accessed | tf_op | source)
XLA Modules:
  0.0 907.5 jit_solution(2537009332283818978)
XLA Ops:
  7.2 0.0 copy-start
  7.2 0.0 copy-start.1
  7.2 0.0 all-reduce.3.cloned.1.call-start
  7.2 2.7 fusion.18
  9.9 0.0 copy-done
  9.9 0.0 copy-done.1
  9.9 3.1 fusion.5
  13.0 3.9 convolution_add_fusion.1
  16.9 2.5 fusion.4
  19.4 0.0 all-reduce.3.cloned.1.call-update
  19.4 0.0 all-reduce.5.cloned.1.call-start
  19.5 350.0 %all-reduce.3.cloned.1.call-done = f32[3584,32]{0,1:T(8,128)} async-done(((f32[3584,32]{0,1:T(8,128)}), f32[3584,32]{0,1:T(8,128)}) %all-reduce.3.cloned.1.call-update) | async-done | bytes 458768 | tf_op jit(solution)/shard_map/psum | solution.py:29
  369.5 1.7 fusion.19
  371.2 22.5 %psum.22 = f32[32,32]{0,1:T(8,128)S(1)} all-reduce(f32[32,32]{0,1:T(8,128)S(1)} %fusion.19), channel_id=1, replica_groups=mesh['dp'=128,'tensor'=8] {'tensor'}, use_global_device_ids=true, to_apply=%region_1.0 | all-reduce | flops 1024 | bytes 8192 | tf_op jit(solution)/shard_map/psum | solution.py:30
  393.6 0.1 copy.9
  393.7 2.9 cholesky.16
  396.7 0.6 compare_reduce_fusion
  397.3 0.7 fusion.15
  398.0 2.4 custom-call.7
  400.4 1.6 convolution_multiply_fusion
  402.0 0.0 copy-start.2
  402.0 0.8 copy-done.2
  402.8 1.5 fusion.20
  404.3 3.5 fusion.6
  407.9 2.1 fusion.21
  409.9 4.8 fusion.2
  414.8 0.0 all-reduce.5.cloned.1.call-update
  414.8 484.5 %all-reduce.5.cloned.1.call-done = f32[8192,32]{0,1:T(8,128)} async-done(((f32[8192,32]{0,1:T(8,128)}), f32[8192,32]{0,1:T(8,128)}) %all-reduce.5.cloned.1.call-update) | async-done | bytes 1048592 | tf_op jit(solution)/shard_map/psum | solution.py:44
  899.3 1.4 dynamic-slice_multiply_fusion
  (2 shorter events, 0.0 us)
Async XLA Ops:
  7.2 2.7 copy-start
  7.2 2.7 copy-start.1
  7.2 362.3 %all-reduce.3.cloned.1.call-start = ((), (), s32[]{:S(2)}) async-start(), calls=%async_computation | async-start | bytes 917504 | tf_op jit(solution)/shard_map/psum | solution.py:29
  19.4 879.8 %all-reduce.5.cloned.1.call-start = ((), (), s32[]{:S(2)}) async-start(), calls=%async_computation.1 | async-start | bytes 2097152 | tf_op jit(solution)/shard_map/psum | solution.py:44
  402.0 0.8 copy-start.2
Sparse Core Ops, SparseCore 0:
  19.6 349.8 all-reduce.2
  414.9 484.2 all-reduce.4
where the time goes:
time: 908 us; the launch traced here: 907 us
  waiting for transfers between devices  834 us (92%)
  matrix products  27.4 us (3%)
  blocking collectives  22.5 us (2%)
  between operations  14.1 us (2%)
    psum x1, waiting for transfers between devices, on_device(): summed_all = lax.psum(local_q, ('dp', 'tensor'))  484 us
    psum x1, waiting for transfers between devices, on_device(): p_mean = lax.psum(local_p, 'dp')  350 us
    psum x1, blocking collectives, on_device(): lax.psum(jnp.dot(p_mean.T, p_mean, precision=highest), 'tensor')  22.5 us
  transfers between devices with their start and end apart: 2, of which 2 were waited for; matrix products, arithmetic and copies ran while one was open for 0% of the time, Pallas kernels for 0%

commit v1 on v0

v1 whole, which is shorter than its diff:
```python
import jax
import jax.numpy as jnp
from jax import lax
from jax.experimental import pallas as pl
from jax.experimental.pallas import tpu as pltpu
from jax.sharding import PartitionSpec as P

MESH = pl.DeviceIdType.MESH
F32, BF16 = jnp.float32, jnp.bfloat16
HIGHEST = lax.Precision.HIGHEST
NT = (((1,), (1,)), ((), ()))
NN = (((1,), (0,)), ((), ()))

NX, NY, NZ, NC = 4, 8, 16, 2
R = 32
FF_ALL, FF, D, TOK = 28672, 3584, 8192, 128
REPLICAS = NX * NZ * NC
HALF = FF // NC
TILES = HALF // 128
G_CHUNKS = 4


def dot(a, b, dims, precision=None):
    return lax.dot_general(a, b, dims, precision=precision, preferred_element_type=F32)


def three_terms(v):
    a = v.astype(BF16).astype(F32)
    r = v - a
    b = r.astype(BF16).astype(F32)
    return a, b, r - b


def inverse_cholesky(gram):
    rows = lax.broadcasted_iota(jnp.int32, (R, 128), 0)
    lanes = lax.broadcasted_iota(jnp.int32, (R, 128), 1)
    m = jnp.where(lanes < R, gram, jnp.where(lanes - R == rows, 1.0, 0.0))
    for k in range(R):
        pivot = m[k : k + 1, k : k + 1]
        inv = lax.rsqrt(pivot)
        inv = inv * (1.5 - 0.5 * pivot * inv * inv)
        row = m[k : k + 1, :] * inv
        column = m[:, k : k + 1] * inv
        m = jnp.where(rows > k, m - column * row, jnp.where(rows == k, row, m))
    return m[:, R : 2 * R]


def kernel(
    hidden, out_grad, prev_hidden, prev_grad, basis_t, warm_t,
    new_basis_t, new_factor_t,
    hid, grad, pb, warm, warm_low,
    s_core, own, r_core, s_x, r_x, s_z, r_z, corr, full, own_tile,
    s_y, r_y, gram_all, s_q, r_qc, s_qx, r_qx, s_qz, r_qz, s_f, r_f, basis_out,
    load_sem, out_sem, send, recv,
):
    dp, y = lax.axis_index("dp"), lax.axis_index("tensor")
    core = lax.rem(dp, NC)
    z = lax.rem(dp // NC, NZ)
    x = dp // (NC * NZ)
    other = 1 - core

    def at(px, pz, pc, py):
        return ((px * NZ + pz) * NC + pc, py)

    partner = at(x, z, other, y)
    x_peers = [at(lax.rem(x + k, NX), z, core, y) for k in range(1, NX)]

    def remote(phase, src, dst, device):
        return pltpu.make_async_remote_copy(
            src_ref=src, dst_ref=dst, send_sem=send.at[phase], recv_sem=recv.at[phase],
            device_id=device, device_id_type=MESH,
        )

    def wait_on(sem, ref):
        pltpu.make_async_copy(ref, ref, sem).wait()

    loads = [pltpu.make_async_copy(warm_t, warm, load_sem.at[0])]
    width = D // G_CHUNKS
    for j in range(G_CHUNKS):
        cols = pl.ds(j * width, width)
        for s, g in enumerate((out_grad, prev_grad)):
            loads.append(
                pltpu.make_async_copy(g.at[:, cols], grad.at[s, :, cols], load_sem.at[1 + 2 * j + s])
            )
    n = 1 + 2 * G_CHUNKS
    loads.append(pltpu.make_async_copy(hidden, hid.at[pl.ds(0, TOK), :], load_sem.at[n]))
    loads.append(pltpu.make_async_copy(prev_hidden, hid.at[pl.ds(TOK, TOK), :], load_sem.at[n + 1]))
    loads.append(pltpu.make_async_copy(basis_t, pb, load_sem.at[n + 2]))
    for copy in loads:
        copy.start()

    barrier = pltpu.get_barrier_semaphore()

    def greet(device):
        pl.semaphore_signal(barrier, inc=1, device_id=device, device_id_type=MESH)

    greet(partner)
    for device in x_peers:
        greet(device)
    for k in range(1, NZ):
        greet(at(x, lax.rem(z + k, NZ), core, y))
    for k in range(1, NY):
        greet(at(x, z, core, lax.rem(y + k, NY)))
        greet(at(x, z, other, lax.rem(y + k, NY)))

    loads[0].wait()
    warm_low[...] = warm[...].astype(BF16)
    acc = [jnp.zeros((R, TOK), F32), jnp.zeros((R, TOK), F32)]
    for j in range(G_CHUNKS):
        cols = slice(j * width, (j + 1) * width)
        for s in range(2):
            loads[1 + 2 * j + s].wait()
            acc[s] = acc[s] + dot(warm_low[:, cols], grad[s, :, cols], NT)
    projected = jnp.concatenate(acc, axis=1).astype(BF16)

    loads[n].wait()
    loads[n + 1].wait()
    my_half = pl.ds(pl.multiple_of(core * HALF, 128), HALF)
    other_half = pl.ds(pl.multiple_of(other * HALF, 128), HALF)
    s_core[...] = dot(projected, hid[:, other_half], NN)
    pl.semaphore_wait(barrier, 1 + (NX - 1) + (NZ - 1) + 2 * (NY - 1))
    remote(0, s_core, r_core, partner).start()
    own[...] = dot(projected, hid[:, my_half], NN)
    wait_on(recv.at[0], r_core)
    s_x[...] = own[...] + r_core[...]

    for k in range(1, NX):
        group = pl.ds(pl.multiple_of(lax.rem(x + k, NX) * 8, 8), 8)
        remote(1, s_x.at[group, :], r_x.at[k - 1], x_peers[k - 1]).start()
    wait_on(recv.at[1], r_x)
    my_rows = pl.ds(pl.multiple_of(x * 8, 8), 8)
    summed = s_x[my_rows, :] + r_x[0] + r_x[1] + r_x[2]
    for j in range(TILES):
        s_z[j] = summed[:, 128 * j : 128 * (j + 1)]

    owner = z < TILES
    for k in range(1, NZ):
        target = lax.rem(z + k, NZ)

        @pl.when(target < TILES)
        def _():
            remote(2, s_z.at[target], r_z.at[k - 1], at(x, target, core, y)).start()

    loads[n + 2].wait()
    tile = jnp.minimum(z, TILES - 1)
    my_tile = pl.ds(pl.multiple_of(core * HALF + tile * 128, 128), 128)
    coupling = dot(warm[...], warm[...], NT, HIGHEST)
    corr[...] = dot(coupling, pb[:, my_tile], NN, HIGHEST)

    @pl.when(owner)
    def _():
        wait_on(recv.at[2], r_z)
        total = s_z[z]
        for k in range(NZ - 1):
            total = total + r_z[k]
        own_tile[...] = total * (1.0 / REPLICAS) - corr[my_rows, :]
        full[my_rows, my_tile] = own_tile[...]
        for k in range(1, NZ):
            target = lax.rem(z + k, NZ)
            remote(3, own_tile, full.at[my_rows, my_tile], at(x, target, core, y)).start()
        wait_on(recv.at[3], full.at[pl.ds(0, 8), pl.ds(0, 128 * (TILES - 1))])

    @pl.when(jnp.logical_not(owner))
    def _():
        wait_on(recv.at[3], full.at[pl.ds(0, 8), pl.ds(0, 128 * TILES)])

    piece = full.at[my_rows, my_half]
    for device in x_peers:
        remote(4, piece, piece, device).start()
    wait_on(recv.at[4], r_x)
    mine = full.at[:, my_half]
    remote(5, mine, mine, partner).start()

    def pulled_half(cols):
        terms = jnp.concatenate(three_terms(full[:, cols]), axis=0).astype(BF16)
        return dot(terms, hid[:, cols], NT)

    zt = pulled_half(my_half)
    wait_on(recv.at[5], r_core)
    zt = zt + pulled_half(other_half)
    zt = zt[0:R] + zt[R : 2 * R] + zt[2 * R : 3 * R]

    for g in range(4):
        for s in range(2):
            s_y[2 * g + s] = zt[8 * g : 8 * (g + 1), 128 * s : 128 * (s + 1)]
    y_peers = [lax.rem(y + k, NY) for k in range(1, NY)]
    for k in range(1, NY):
        target = y_peers[k - 1]
        remote(6, s_y.at[target], r_y.at[k - 1], at(x, z, core, target)).start()

    p_t = full[...]
    gram = dot(p_t, p_t, NT, HIGHEST)
    cross = dot(p_t, pb[...], NT, HIGHEST)
    gram_all[y] = jnp.concatenate([gram, cross, jnp.zeros((R, 128 - 2 * R), F32)], axis=1)
    for k in range(1, NY):
        remote(7, gram_all.at[y], gram_all.at[y], at(x, z, core, y_peers[k - 1])).start()

    wait_on(recv.at[6], r_y)
    z_tile = s_y[y]
    for k in range(NY - 1):
        z_tile = z_tile + r_y[k]

    terms = jnp.concatenate((*three_terms(z_tile), jnp.zeros((8, 128), F32)), axis=0).astype(BF16)
    q = dot(terms, grad[lax.rem(y, 2)], NN)
    q = q[0:8] + q[8:16] + q[16:24]
    for px in range(NX):
        for k in range(NZ // 2):
            for pc in range(NC):
                t = px * NZ + 2 * k + pc
                s_q[pc, px, k] = q[:, 128 * t : 128 * (t + 1)]

    remote(8, s_q.at[other], r_qc, partner).start()
    wait_on(recv.at[8], r_qc)
    s_qx[...] = s_q[core] + r_qc[...]
    for k in range(1, NX):
        remote(9, s_qx.at[lax.rem(x + k, NX)], r_qx.at[k - 1], x_peers[k - 1]).start()
    wait_on(recv.at[9], r_qx)
    s_qz[...] = s_qx[x] + r_qx[0] + r_qx[1] + r_qx[2]

    keeps = lax.rem(z, 2) == core
    for j in range(NZ // 2):
        target = lax.rem(z + lax.rem(z + core, 2) + 2 * j, NZ)
        slot = lax.rem(z - target + NZ, NZ) - 1

        @pl.when(target != z)
        def _():
            remote(10, s_qz.at[target // 2], r_qz.at[slot], at(x, target, core, y)).start()

    wait_on(recv.at[7], gram_all.at[pl.ds(0, NY - 1)])
    sums = gram_all[0]
    for k in range(1, NY):
        sums = sums + gram_all[k]
    inverse = inverse_cholesky(sums)
    cross_all = sums[:, R : 2 * R]
    scaled = inverse * jnp.sqrt(F32(FF_ALL))
    basis_out[...] = dot(scaled, full[...], NN, HIGHEST)
    out_copy = pltpu.make_async_copy(basis_out, new_basis_t, out_sem)
    out_copy.start()
    col_tile = pl.ds(pl.multiple_of((x * NZ + z) * 128, 128), 128)
    taken = dot(cross_all, warm[:, col_tile], NN, HIGHEST)

    @pl.when(keeps)
    def _():
        wait_on(recv.at[10], r_qz)
        total = s_qz[z // 2]
        for k in range(NZ - 1):
            total = total + r_qz[k]
        s_f[...] = total
        r_f[y] = total
        remote(11, s_f, r_f.at[y], partner).start()
        for k in range(1, NY):
            for pc in (core, other):
                remote(11, s_f, r_f.at[y], at(x, z, pc, y_peers[k - 1])).start()
        wait_on(recv.at[11], r_f.at[pl.ds(0, NY - 1)])

    @pl.when(jnp.logical_not(keeps))
    def _():
        wait_on(recv.at[11], r_f)

    q_t = jnp.concatenate([r_f[2 * g] + r_f[2 * g + 1] for g in range(4)], axis=0)
    result = dot(inverse, q_t * (1.0 / REPLICAS) - taken, NN, HIGHEST)
    new_factor_t[...] = jnp.where(core == 0, result[:, 0:64], result[:, 64:128])

    wait_on(send.at[0], s_core)
    wait_on(send.at[1], r_x)

    @pl.when(owner)
    def _():
        wait_on(send.at[2], s_z.at[pl.ds(0, TILES - 1)])
        wait_on(send.at[3], r_z)

    @pl.when(jnp.logical_not(owner))
    def _():
        wait_on(send.at[2], s_z)

    wait_on(send.at[4], r_x)
    wait_on(send.at[5], r_core)
    wait_on(send.at[6], r_y)
    wait_on(send.at[7], gram_all.at[pl.ds(0, NY - 1)])
    wait_on(send.at[8], r_qc)
    wait_on(send.at[9], r_qx)

    @pl.when(keeps)
    def _():
        wait_on(send.at[10], s_qz.at[pl.ds(0, NZ // 2 - 1)])
        wait_on(send.at[11], r_qz)

    @pl.when(jnp.logical_not(keeps))
    def _():
        wait_on(send.at[10], s_qz)

    out_copy.wait()


def on_device(hidden, out_grad, prev_hidden, prev_grad, prev_basis, warm_start):
    hbm = pl.BlockSpec(memory_space=pl.ANY)
    vmem = pltpu.VMEM
    dma = pltpu.SemaphoreType.DMA
    new_basis_t, new_factor_t = pl.pallas_call(
        kernel,
        out_shape=(
            jax.ShapeDtypeStruct((R, FF), F32),
            jax.ShapeDtypeStruct((R, D // REPLICAS), F32),
        ),
        in_specs=[hbm] * 6,
        out_specs=(hbm, pl.BlockSpec(memory_space=pltpu.VMEM)),
        scratch_shapes=[
            vmem((2 * TOK, FF), BF16),
            vmem((2, TOK, D), BF16),
            vmem((R, FF), F32),
            vmem((R, D), F32),
            vmem((R, D), BF16),
            vmem((R, HALF), F32),
            vmem((R, HALF), F32),
            vmem((R, HALF), F32),
            vmem((R, HALF), F32),
            vmem((NX - 1, 8, HALF), F32),
            vmem((TILES, 8, 128), F32),
            vmem((NZ - 1, 8, 128), F32),
            vmem((R, 128), F32),
            vmem((R, FF), F32),
            vmem((8, 128), F32),
            vmem((NY, 8, 128), F32),
            vmem((NY - 1, 8, 128), F32),
            vmem((NY, R, 128), F32),
            vmem((NC, NX, NZ // 2, 8, 128), F32),
            vmem((NX, NZ // 2, 8, 128), F32),
            vmem((NX, NZ // 2, 8, 128), F32),
            vmem((NX - 1, NZ // 2, 8, 128), F32),
            vmem((NZ // 2, 8, 128), F32),
            vmem((NZ - 1, 8, 128), F32),
            vmem((8, 128), F32),
            vmem((NY, 8, 128), F32),
            vmem((R, FF), F32),
            dma((4 + 2 * G_CHUNKS,)),
            dma,
            dma((12,)),
            dma((12,)),
        ],
        compiler_params=pltpu.CompilerParams(collective_id=0, has_side_effects=True),
        name="powersgd",
    )(hidden, out_grad, prev_hidden, prev_grad, prev_basis.T, warm_start.T)
    return new_basis_t.T, new_factor_t.T


def solution(mesh):
    return jax.shard_map(
        on_device,
        mesh=mesh,
        in_specs=(
            P("dp", "tensor"),
            P("dp", None),
            P("dp", "tensor"),
            P("dp", None),
            P("tensor", None),
            P(),
        ),
        out_specs=(P("tensor", None), P("dp", None)),
        check_vma=False,
    )
```

time: 908 us -> 78.2 us (0.09)
  waiting for transfers between devices: 834 us -> 0 us
  Pallas kernels: 0 us -> 74.2 us
  matrix products: 27.4 us -> 0 us
  blocking collectives: 22.5 us -> 0 us
  between operations: 14.1 us -> 0.64 us
    psum x2 -> x0, waiting for transfers between devices: 834 us -> none  [the longest x1 484 us: on_device(): summed_all = lax.psum(local_q, ('dp', 'tensor'))]
    pallas_call x0 -> x1, Pallas kernels: none -> 74.2 us  [on_device(): pl.pallas_call(kernel, out_shape=(jax.ShapeDtypeStruct((R, FF), F32), jax...]
    dot_general x9 -> x0, matrix products: 25.8 us -> none  [the longest x1 4.84 us: on_device(): jnp.einsum('td,tr->dr', prev_grad, pulled_prev, preferred_element_type=jn...]
    psum x1 -> x0, blocking collectives: 22.5 us -> none  [on_device(): lax.psum(jnp.dot(p_mean.T, p_mean, precision=highest), 'tensor')]
  transfers between devices with their start and end apart: 2 -> 0, of which waited for: 2 -> 0; matrix products, arithmetic and copies ran while one was open for 0% -> 0% of each run, Pallas kernels for 0% -> 0%
where the time goes in v1:
time: 78.2 us; the launch traced here: 77.9 us
  Pallas kernels  74.2 us (95%)
  local copies, waits for them, and re-layouts  3.14 us (4%)
    pallas_call x1, Pallas kernels, on_device(): pl.pallas_call(kernel, out_shape=(jax.ShapeDtypeStruct((R, FF), F32), jax...  74.2 us
    unnamed x2, local copies, waits for them, and re-layouts  3.14 us

profile of v1, /device:TPU:1, one launch (start us, length us, event | category | flops | bytes accessed | tf_op | source)
XLA Modules:
  0.0 77.9 jit_solution(16724871853293523312)
XLA Ops:
  0.6 74.2 %powersgd.1 = (f32[32,3584]{1,0:T(8,128)}, f32[32,64]{1,0:T(8,128)}) custom-call(bf16[128,3584]{1,0:T(8,128)(2,1)} %hidden.1, bf16[128,8192]{1,0:T(8,128)(2,1)} %out_grad.1, bf16[128,3584]{1,0:T(8,128)(2,1)} %prev_hidden.1, bf16[128,8192]{1,0:T(8,128)(2,1)} %prev_grad.1, f32[32,3584]{1,0:T(8,128)} %bitcast.6, f32[32,8192]{1,0:T(8,128)} %bitcast.4), custom_call_target="tpu_custom_call" | custom-call | tf_op jit(solution)/shard_map/powersgd/pallas_call | solution.py:299
  74.8 1.8 %copy.10 = f32[3584,32]{0,1:T(8,128)} copy(f32[3584,32]{0,1:T(8,128)} %bitcast.5) | data formatting | bytes 917504
  76.6 1.3 %copy.11 = f32[64,32]{0,1:T(8,128)} copy(f32[64,32]{0,1:T(8,128)} %bitcast.7) | data formatting | bytes 16384

commit v2 on v1

v2 whole, which is shorter than its diff:
```python
import jax
import jax.numpy as jnp
from jax import lax
from jax.experimental import pallas as pl
from jax.experimental.pallas import tpu as pltpu
from jax.sharding import PartitionSpec as P

MESH = pl.DeviceIdType.MESH
F32, BF16 = jnp.float32, jnp.bfloat16
HIGHEST = lax.Precision.HIGHEST
NT = (((1,), (1,)), ((), ()))
NN = (((1,), (0,)), ((), ()))

NX, NY, NZ, NC = 4, 8, 16, 2
R = 32
FF_ALL, FF, D, TOK = 28672, 3584, 8192, 128
REPLICAS = NX * NZ * NC
HALF = FF // NC
TILES = HALF // 128
G_CHUNKS = 4


def dot(a, b, dims, precision=None):
    return lax.dot_general(a, b, dims, precision=precision, preferred_element_type=F32)


def three_terms(v):
    a = v.astype(BF16).astype(F32)
    r = v - a
    b = r.astype(BF16).astype(F32)
    return a, b, r - b


def inverse_cholesky(gram):
    rows = lax.broadcasted_iota(jnp.int32, (R, 128), 0)
    lanes = lax.broadcasted_iota(jnp.int32, (R, 128), 1)
    m = jnp.where(lanes < R, gram, jnp.where(lanes - R == rows, 1.0, 0.0))
    for k in range(R):
        pivot = m[k : k + 1, k : k + 1]
        inv = lax.rsqrt(pivot)
        inv = inv * (1.5 - 0.5 * pivot * inv * inv)
        row = m[k : k + 1, :] * inv
        column = m[:, k : k + 1] * inv
        m = jnp.where(rows > k, m - column * row, jnp.where(rows == k, row, m))
    return m[:, R : 2 * R]


Z_FAR = (8, 7, 9, 6, 10, 5, 11, 4, 12, 3, 13, 2, 14, 1, 15)
Z_EVEN = (8, 10, 6, 12, 4, 14, 2, 16)
Y_FAR = (4, 3, 5, 2, 6, 1, 7)
X_FAR = (2, 1, 3)


def kernel(
    hidden, out_grad, prev_hidden, prev_grad, basis_t, warm_t,
    new_basis_t, new_factor_t,
    hid, grad, pb, pb_low, warm, warm_low,
    s_core, own, r_core, s_x, r_x0, r_x1, s_z, r_z, corr, full, low,
    s_y, r_y, gram_all, s_q, o_q, r_qc, s_qx, r_qx, s_qz, r_qz, s_f, r_f,
    load_sem, send, recv, owner_sem,
):
    dp, y = lax.axis_index("dp"), lax.axis_index("tensor")
    core = lax.rem(dp, NC)
    z = lax.rem(dp // NC, NZ)
    x = dp // (NC * NZ)
    other = 1 - core
    odd = lax.rem(z, 2)
    owner = jnp.logical_and(odd == 0, z < TILES)
    keeps = odd == core

    def at(px, pz, pc, py):
        return ((px * NZ + pz) * NC + pc, py)

    partner = at(x, z, other, y)
    x_peer = {k: at(lax.rem(x + k, NX), z, core, y) for k in X_FAR}
    evens = [lax.rem(z + a - odd, NZ) for a in Z_EVEN]

    def remote(phase, src, dst, device, recv_sem=None):
        return pltpu.make_async_remote_copy(
            src_ref=src, dst_ref=dst, send_sem=send.at[phase],
            recv_sem=recv.at[phase] if recv_sem is None else recv_sem,
            device_id=device, device_id_type=MESH,
        )

    def wait_on(sem, ref):
        pltpu.make_async_copy(ref, ref, sem).wait()

    def row_group(g):
        return pl.ds(pl.multiple_of(g * 8, 8), 8)

    loads = [pltpu.make_async_copy(warm_t, warm, load_sem.at[0])]
    width = D // G_CHUNKS
    for j in range(G_CHUNKS):
        cols = pl.ds(j * width, width)
        for s, g in enumerate((out_grad, prev_grad)):
            loads.append(
                pltpu.make_async_copy(g.at[:, cols], grad.at[s, :, cols], load_sem.at[1 + 2 * j + s])
            )
    n = 1 + 2 * G_CHUNKS
    loads.append(pltpu.make_async_copy(hidden, hid.at[pl.ds(0, TOK), :], load_sem.at[n]))
    loads.append(pltpu.make_async_copy(prev_hidden, hid.at[pl.ds(TOK, TOK), :], load_sem.at[n + 1]))
    loads.append(pltpu.make_async_copy(basis_t, pb, load_sem.at[n + 2]))
    for copy in loads:
        copy.start()

    barrier = pltpu.get_barrier_semaphore()

    def greet(device):
        pl.semaphore_signal(barrier, inc=1, device_id=device, device_id_type=MESH)

    greet(partner)
    for k in X_FAR:
        greet(x_peer[k])

    @pl.when(owner)
    def _():
        for k in Z_FAR:
            greet(at(x, lax.rem(z + k, NZ), core, y))

    for k in Y_FAR:
        greet(at(x, z, core, lax.rem(y + k, NY)))
        greet(at(x, z, other, lax.rem(y + k, NY)))

    loads[0].wait()
    warm_low[...] = warm[...].astype(BF16)
    acc = [jnp.zeros((R, TOK), F32), jnp.zeros((R, TOK), F32)]
    for j in range(G_CHUNKS):
        cols = slice(j * width, (j + 1) * width)
        for s in range(2):
            loads[1 + 2 * j + s].wait()
            acc[s] = acc[s] + dot(warm_low[:, cols], grad[s, :, cols], NT)
    projected = jnp.concatenate(acc, axis=1).astype(BF16)

    loads[n].wait()
    loads[n + 1].wait()
    my_half = pl.ds(pl.multiple_of(core * HALF, 128), HALF)
    chunks = ((0, 1024), (1024, HALF - 1024))
    for i, (start, size) in enumerate(chunks):
        there = pl.ds(pl.multiple_of(other * HALF + start, 128), size)
        here = pl.ds(start, size)
        s_core[:, here] = dot(projected, hid[:, there], NN)
        if i == 0:
            pl.semaphore_wait(barrier, 1 + (NX - 1) + 2 * (NY - 1) + TILES // 2 - owner.astype(jnp.int32))
        remote(i, s_core.at[:, here], r_core.at[:, here], partner).start()
    r_x = (r_x0, r_x1)
    for i, (start, size) in enumerate(chunks):
        mine = pl.ds(pl.multiple_of(core * HALF + start, 128), size)
        here = pl.ds(start, size)
        own[:, here] = dot(projected, hid[:, mine], NN)
        wait_on(recv.at[i], r_core.at[:, here])
        s_x[:, here] = own[:, here] + r_core[:, here]
        for k in X_FAR:
            remote(2 + i, s_x.at[row_group(lax.rem(x + k, NX)), here], r_x[i].at[k - 1], x_peer[k]).start()

    my_rows = row_group(x)
    for i, (start, size) in enumerate(chunks):
        wait_on(recv.at[2 + i], r_x[i])
        summed = s_x[my_rows, start : start + size] + r_x[i][0] + r_x[i][1] + r_x[i][2]
        for j in range(size // 256):
            s_z[start // 256 + j] = summed[:, 256 * j : 256 * (j + 1)]
        last = (start + size) // 128
        for target in evens:
            @pl.when(jnp.logical_and(target != z, jnp.logical_and(target >= start // 128, target < last)))
            def _():
                slot = lax.rem(z - target + NZ, NZ) - 1
                remote(4, s_z.at[target // 2], r_z.at[slot], at(x, target, core, y)).start()

    loads[n + 2].wait()
    pair = pl.ds(pl.multiple_of(core * HALF + jnp.minimum(z, TILES - 2) // 2 * 256, 256), 256)

    @pl.when(owner)
    def _():
        coupling = dot(warm[...], warm[...], NT, HIGHEST)
        corr[...] = dot(coupling, pb[:, pair], NN, HIGHEST)
        wait_on(recv.at[4], r_z)
        total = s_z[z // 2]
        for k in range(NZ - 1):
            total = total + r_z[k]
        full[my_rows, pair] = total * (1.0 / REPLICAS) - corr[my_rows, :]
        tiles = full.at[my_rows, pair]
        for k in Z_FAR:
            remote(5, tiles, tiles, at(x, lax.rem(z + k, NZ), core, y), owner_sem.at[z // 2]).start()
        for k in X_FAR:
            remote(6, tiles, tiles, x_peer[k], recv.at[5 + k]).start()

    pb_low[...] = jnp.concatenate(three_terms(pb[...]), axis=0).astype(BF16)

    for target in reversed(evens):
        @pl.when(jnp.logical_and(target != z, target < TILES))
        def _():
            tiles = full.at[my_rows, pl.ds(pl.multiple_of(core * HALF + target // 2 * 256, 256), 256)]
            wait_on(owner_sem.at[target // 2], tiles)
            for k in X_FAR:
                remote(6, tiles, tiles, x_peer[k], recv.at[5 + k]).start()

    piece = full.at[my_rows, my_half]
    remote(7, piece, piece, partner, recv.at[9]).start()
    for k in (1, 3, 2):
        piece = full.at[row_group(lax.rem(x - k + NX, NX)), my_half]
        wait_on(recv.at[5 + k], piece)
        remote(7, piece, piece, partner, recv.at[9]).start()

    def pulled_half(cols):
        low[:, cols] = jnp.concatenate(three_terms(full[:, cols]), axis=0).astype(BF16)
        return dot(low[:, cols], hid[:, cols], NT)

    zt = pulled_half(my_half)
    wait_on(recv.at[9], r_core)
    zt = zt + pulled_half(pl.ds(pl.multiple_of(other * HALF, 128), HALF))
    zt = zt[0:R] + zt[R : 2 * R] + zt[2 * R : 3 * R]

    for g in range(4):
        for s in range(2):
            s_y[2 * g + s] = zt[8 * g : 8 * (g + 1), 128 * s : 128 * (s + 1)]
    y_peer = {k: lax.rem(y + k, NY) for k in Y_FAR}
    for k in Y_FAR:
        remote(8, s_y.at[y_peer[k]], r_y.at[k - 1], at(x, z, core, y_peer[k]), recv.at[10]).start()

    def folded(m):
        m = m[0:R] + m[R : 2 * R] + m[2 * R : 3 * R]
        return m[:, 0:R] + m[:, R : 2 * R] + m[:, 2 * R : 3 * R]

    gram = folded(dot(low[...], low[...], NT))
    cross = folded(dot(low[...], pb_low[...], NT))
    gram_all[y] = jnp.concatenate([gram, cross, jnp.zeros((R, 128 - 2 * R), F32)], axis=1)
    for k in Y_FAR:
        remote(9, gram_all.at[y], gram_all.at[y], at(x, z, core, y_peer[k]), recv.at[11]).start()

    wait_on(recv.at[10], r_y)
    z_tile = s_y[y]
    for k in range(NY - 1):
        z_tile = z_tile + r_y[k]

    terms = jnp.concatenate((*three_terms(z_tile), jnp.zeros((8, 128), F32)), axis=0).astype(BF16)
    tokens = lax.rem(y, 2)
    block = NZ * 128

    def right_block(k):
        cols = pl.ds(pl.multiple_of(lax.rem(x + k, NX) * block, block), block)
        q = dot(terms, grad[tokens, :, cols], NN)
        q = q[0:8] + q[8:16] + q[16:24]
        for j in range(NZ // 2):
            even = q[:, 256 * j : 256 * j + 128]
            uneven = q[:, 256 * j + 128 : 256 * (j + 1)]
            s_q[k, j] = jnp.where(core == 0, uneven, even)
            o_q[k, j] = jnp.where(core == 0, even, uneven)
        remote(12 + k, s_q.at[k], r_qc.at[k], partner).start()

    def pass_on(k):
        wait_on(recv.at[12 + k], r_qc.at[k])
        s_qx[k] = o_q[k] + r_qc[k]
        if k:
            remote(10, s_qx.at[k], r_qx.at[k - 1], x_peer[k], recv.at[16]).start()

    right_block(2)
    right_block(1)
    right_block(3)
    pass_on(2)
    right_block(0)
    pass_on(1)
    pass_on(3)
    pass_on(0)
    wait_on(recv.at[16], r_qx)
    s_qz[...] = s_qx[0] + r_qx[0] + r_qx[1] + r_qx[2]

    for a in Z_EVEN:
        target = lax.rem(z + a - lax.rem(z + core, 2), NZ)
        slot = lax.rem(z - target + NZ, NZ) - 1

        @pl.when(target != z)
        def _():
            remote(11, s_qz.at[target // 2], r_qz.at[slot], at(x, target, core, y), recv.at[17]).start()

    wait_on(recv.at[11], gram_all.at[pl.ds(0, NY - 1)])
    sums = gram_all[0]
    for k in range(1, NY):
        sums = sums + gram_all[k]
    inverse = inverse_cholesky(sums)
    cross_all = sums[:, R : 2 * R]
    scaled = inverse * jnp.sqrt(F32(FF_ALL))
    new_basis_t[...] = dot(scaled, full[...], NN, HIGHEST)
    col_tile = pl.ds(pl.multiple_of((x * NZ + z) * 128, 128), 128)
    taken = dot(cross_all, warm[:, col_tile], NN, HIGHEST)

    @pl.when(keeps)
    def _():
        wait_on(recv.at[17], r_qz)
        total = s_qz[z // 2]
        for k in range(NZ - 1):
            total = total + r_qz[k]
        s_f[...] = total
        r_f[y] = total
        for k in Y_FAR:
            for pc in (core, other):
                remote(16, s_f, r_f.at[y], at(x, z, pc, y_peer[k]), recv.at[18]).start()
        remote(16, s_f, r_f.at[y], partner, recv.at[18]).start()
        wait_on(recv.at[18], r_f.at[pl.ds(0, NY - 1)])

    @pl.when(jnp.logical_not(keeps))
    def _():
        wait_on(recv.at[18], r_f)

    q_t = jnp.concatenate([r_f[2 * g] + r_f[2 * g + 1] for g in range(4)], axis=0)
    result = dot(inverse, q_t * (1.0 / REPLICAS) - taken, NN, HIGHEST)
    new_factor_t[...] = jnp.where(core == 0, result[:, 0:64], result[:, 64:128])

    for i, (start, size) in enumerate(chunks):
        wait_on(send.at[i], s_core.at[:, pl.ds(start, size)])
        wait_on(send.at[2 + i], r_x[i])

    @pl.when(owner)
    def _():
        wait_on(send.at[4], s_z.at[pl.ds(0, TILES // 2 - 1)])
        wait_on(send.at[5], r_z)

    @pl.when(jnp.logical_not(owner))
    def _():
        wait_on(send.at[4], s_z)

    wait_on(send.at[6], own.at[pl.ds(0, 24), :])
    wait_on(send.at[7], r_core)
    wait_on(send.at[8], r_y)
    wait_on(send.at[9], gram_all.at[pl.ds(0, NY - 1)])
    wait_on(send.at[10], r_qx)
    for k in range(NX):
        wait_on(send.at[12 + k], r_qc.at[k])

    @pl.when(keeps)
    def _():
        wait_on(send.at[11], s_qz.at[pl.ds(0, NZ // 2 - 1)])
        wait_on(send.at[16], r_qz)

    @pl.when(jnp.logical_not(keeps))
    def _():
        wait_on(send.at[11], s_qz)


def hand_over(basis, factor, new_basis_t, new_factor_t, sem):
    copies = (
        pltpu.make_async_copy(basis, new_basis_t, sem.at[0]),
        pltpu.make_async_copy(factor, new_factor_t, sem.at[1]),
    )
    for copy in copies:
        copy.start()
    for copy in copies:
        copy.wait()


def on_device(hidden, out_grad, prev_hidden, prev_grad, prev_basis, warm_start):
    hbm = pl.BlockSpec(memory_space=pl.ANY)
    vmem = pltpu.VMEM
    dma = pltpu.SemaphoreType.DMA
    results = pl.pallas_call(
        kernel,
        out_shape=(vmem((R, FF), F32), vmem((R, D // REPLICAS), F32)),
        in_specs=[hbm] * 6,
        out_specs=(pl.BlockSpec(memory_space=pltpu.VMEM),) * 2,
        scratch_shapes=[
            vmem((2 * TOK, FF), BF16),
            vmem((2, TOK, D), BF16),
            vmem((R, FF), F32),
            vmem((3 * R, FF), BF16),
            vmem((R, D), F32),
            vmem((R, D), BF16),
            vmem((R, HALF), F32),
            vmem((R, HALF), F32),
            vmem((R, HALF), F32),
            vmem((R, HALF), F32),
            vmem((NX - 1, 8, 1024), F32),
            vmem((NX - 1, 8, HALF - 1024), F32),
            vmem((TILES // 2, 8, 256), F32),
            vmem((NZ - 1, 8, 256), F32),
            vmem((R, 256), F32),
            vmem((R, FF), F32),
            vmem((3 * R, FF), BF16),
            vmem((NY, 8, 128), F32),
            vmem((NY - 1, 8, 128), F32),
            vmem((NY, R, 128), F32),
            vmem((NX, NZ // 2, 8, 128), F32),
            vmem((NX, NZ // 2, 8, 128), F32),
            vmem((NX, NZ // 2, 8, 128), F32),
            vmem((NX, NZ // 2, 8, 128), F32),
            vmem((NX - 1, NZ // 2, 8, 128), F32),
            vmem((NZ // 2, 8, 128), F32),
            vmem((NZ - 1, 8, 128), F32),
            vmem((8, 128), F32),
            vmem((NY, 8, 128), F32),
            dma((4 + 2 * G_CHUNKS,)),
            dma((17,)),
            dma((19,)),
            dma((TILES // 2,)),
        ],
        compiler_params=pltpu.CompilerParams(collective_id=0, has_side_effects=True),
        name="powersgd",
    )(hidden, out_grad, prev_hidden, prev_grad, prev_basis.T, warm_start.T)
    new_basis_t, new_factor_t = pl.pallas_call(
        hand_over,
        out_shape=(jax.ShapeDtypeStruct((R, FF), F32), jax.ShapeDtypeStruct((R, D // REPLICAS), F32)),
        in_specs=[pl.BlockSpec(memory_space=pltpu.VMEM)] * 2,
        out_specs=(hbm, hbm),
        scratch_shapes=[dma((2,))],
        name="hand_over",
    )(*(pltpu.with_memory_space_constraint(r, pltpu.VMEM) for r in results))
    return new_basis_t.T, new_factor_t.T


def solution(mesh):
    return jax.shard_map(
        on_device,
        mesh=mesh,
        in_specs=(
            P("dp", "tensor"),
            P("dp", None),
            P("dp", "tensor"),
            P("dp", None),
            P("tensor", None),
            P(),
        ),
        out_specs=(P("tensor", None), P("dp", None)),
        check_vma=False,
    )
```

time: 78.2 us -> 73 us (0.934)
  local copies, waits for them, and re-layouts: 3.14 us -> 0 us
  Pallas kernels: 74.2 us -> 72.3 us
    unnamed x2 -> x0, local copies, waits for them, and re-layouts: 3.14 us -> none
    pallas_call x1 -> x2, Pallas kernels: 74.2 us -> 72.3 us  [the longest x1 71.5 us: on_device(): pl.pallas_call(kernel, out_shape=(vmem((R, FF), F32), vmem((R, D // REPLI...]
where the time goes in v2:
time: 73 us; the launch traced here: 72.9 us
  Pallas kernels  72.3 us (99%)
    pallas_call x1, Pallas kernels, on_device(): pl.pallas_call(kernel, out_shape=(vmem((R, FF), F32), vmem((R, D // REPLI...  71.5 us

profile of v2, /device:TPU:1, one launch (start us, length us, event | category | flops | bytes accessed | tf_op | source)
XLA Modules:
  0.0 72.9 jit_solution(4495236257205748682)
XLA Ops:
  0.6 71.5 %powersgd.1 = (f32[32,3584]{1,0:T(8,128)S(1)}, f32[32,64]{1,0:T(8,128)S(1)}) custom-call(bf16[128,3584]{1,0:T(8,128)(2,1)} %hidden.1, bf16[128,8192]{1,0:T(8,128)(2,1)} %out_grad.1, bf16[128,3584]{1,0:T(8,128)(2,1)} %prev_hidden.1, bf16[128,8192]{1,0:T(8,128)(2,1)} %prev_grad.1, f32[32,3584]{1,0:T(8,128)} %bitcast.5, f32[32,8192]{1,0:T(8,128)} %bitcast.4), custom_call_target="tpu_custom_call" | custom-call | tf_op jit(solution)/shard_map/powersgd/pallas_call | solution.py:353
  72.1 0.8 %hand_over.1 = (f32[32,3584]{1,0:T(8,128)}, f32[32,64]{1,0:T(8,128)}) custom-call(f32[32,3584]{1,0:T(8,128)S(1)} %get-tuple-element.6.basis, f32[32,64]{1,0:T(8,128)S(1)} %get-tuple-element.7.factor), custom_call_target="tpu_custom_call" | custom-call | tf_op jit(solution)/shard_map/hand_over/pallas_call | solution.py:396

commit v3 on v2

--- a/solution.py
+++ b/solution.py
@@ -46,7 +46,7 @@
 
 
 Z_FAR = (8, 7, 9, 6, 10, 5, 11, 4, 12, 3, 13, 2, 14, 1, 15)
-Z_EVEN = (8, 10, 6, 12, 4, 14, 2, 16)
+Z_PAIR = (8, 10, 6, 12, 4, 14, 2, 16)
 Y_FAR = (4, 3, 5, 2, 6, 1, 7)
 X_FAR = (2, 1, 3)
 
@@ -65,15 +65,21 @@
     x = dp // (NC * NZ)
     other = 1 - core
     odd = lax.rem(z, 2)
-    owner = jnp.logical_and(odd == 0, z < TILES)
     keeps = odd == core
 
     def at(px, pz, pc, py):
         return ((px * NZ + pz) * NC + pc, py)
 
+    def owns(pz):
+        return lax.rem(pz, NZ // 2) != NZ // 2 - 1
+
+    def tile_of(pz):
+        return pz - pz // (NZ // 2)
+
+    owner = owns(z)
     partner = at(x, z, other, y)
     x_peer = {k: at(lax.rem(x + k, NX), z, core, y) for k in X_FAR}
-    evens = [lax.rem(z + a - odd, NZ) for a in Z_EVEN]
+    z_peer = {k: lax.rem(z + k, NZ) for k in Z_FAR}
 
     def remote(phase, src, dst, device, recv_sem=None):
         return pltpu.make_async_remote_copy(
@@ -115,7 +121,7 @@
     @pl.when(owner)
     def _():
         for k in Z_FAR:
-            greet(at(x, lax.rem(z + k, NZ), core, y))
+            greet(at(x, z_peer[k], core, y))
 
     for k in Y_FAR:
         greet(at(x, z, core, lax.rem(y + k, NY)))
@@ -123,13 +129,13 @@
 
     loads[0].wait()
     warm_low[...] = warm[...].astype(BF16)
-    acc = [jnp.zeros((R, TOK), F32), jnp.zeros((R, TOK), F32)]
+    acc = [jnp.zeros((TOK, R), F32), jnp.zeros((TOK, R), F32)]
     for j in range(G_CHUNKS):
         cols = slice(j * width, (j + 1) * width)
         for s in range(2):
             loads[1 + 2 * j + s].wait()
-            acc[s] = acc[s] + dot(warm_low[:, cols], grad[s, :, cols], NT)
-    projected = jnp.concatenate(acc, axis=1).astype(BF16)
+            acc[s] = acc[s] + dot(grad[s, :, cols], warm_low[:, cols], NT)
+    projected = jnp.concatenate([a.T for a in acc], axis=1).astype(BF16)
 
     loads[n].wait()
     loads[n + 1].wait()
@@ -140,7 +146,7 @@
         here = pl.ds(start, size)
         s_core[:, here] = dot(projected, hid[:, there], NN)
         if i == 0:
-            pl.semaphore_wait(barrier, 1 + (NX - 1) + 2 * (NY - 1) + TILES // 2 - owner.astype(jnp.int32))
+            pl.semaphore_wait(barrier, 1 + (NX - 1) + 2 * (NY - 1) + TILES - owner.astype(jnp.int32))
         remote(i, s_core.at[:, here], r_core.at[:, here], partner).start()
     r_x = (r_x0, r_x1)
     for i, (start, size) in enumerate(chunks):
@@ -156,42 +162,48 @@
     for i, (start, size) in enumerate(chunks):
         wait_on(recv.at[2 + i], r_x[i])
         summed = s_x[my_rows, start : start + size] + r_x[i][0] + r_x[i][1] + r_x[i][2]
-        for j in range(size // 256):
-            s_z[start // 256 + j] = summed[:, 256 * j : 256 * (j + 1)]
-        last = (start + size) // 128
-        for target in evens:
-            @pl.when(jnp.logical_and(target != z, jnp.logical_and(target >= start // 128, target < last)))
+        for j in range(size // 128):
+            s_z[start // 128 + j] = summed[:, 128 * j : 128 * (j + 1)]
+        for k in Z_FAR:
+            tile = tile_of(z_peer[k])
+            in_chunk = jnp.logical_and(tile >= start // 128, tile < (start + size) // 128)
+
+            @pl.when(jnp.logical_and(owns(z_peer[k]), in_chunk))
             def _():
-                slot = lax.rem(z - target + NZ, NZ) - 1
-                remote(4, s_z.at[target // 2], r_z.at[slot], at(x, target, core, y)).start()
+                remote(4, s_z.at[tile], r_z.at[NZ - 1 - k], at(x, z_peer[k], core, y)).start()
 
     loads[n + 2].wait()
-    pair = pl.ds(pl.multiple_of(core * HALF + jnp.minimum(z, TILES - 2) // 2 * 256, 256), 256)
+    my_tile = jnp.minimum(tile_of(z), TILES - 1)
+
+    def tile_columns(tile):
+        return pl.ds(pl.multiple_of(core * HALF + tile * 128, 128), 128)
 
     @pl.when(owner)
     def _():
         coupling = dot(warm[...], warm[...], NT, HIGHEST)
-        corr[...] = dot(coupling, pb[:, pair], NN, HIGHEST)
+        corr[...] = dot(coupling, pb[:, tile_columns(my_tile)], NN, HIGHEST)
         wait_on(recv.at[4], r_z)
-        total = s_z[z // 2]
+        total = s_z[my_tile]
         for k in range(NZ - 1):
             total = total + r_z[k]
-        full[my_rows, pair] = total * (1.0 / REPLICAS) - corr[my_rows, :]
-        tiles = full.at[my_rows, pair]
+        full[my_rows, tile_columns(my_tile)] = total * (1.0 / REPLICAS) - corr[my_rows, :]
+        done = full.at[my_rows, tile_columns(my_tile)]
+        for k in X_FAR:
+            remote(6, done, done, x_peer[k], recv.at[5 + k]).start()
         for k in Z_FAR:
-            remote(5, tiles, tiles, at(x, lax.rem(z + k, NZ), core, y), owner_sem.at[z // 2]).start()
-        for k in X_FAR:
-            remote(6, tiles, tiles, x_peer[k], recv.at[5 + k]).start()
+            remote(5, done, done, at(x, z_peer[k], core, y), owner_sem.at[my_tile]).start()
 
     pb_low[...] = jnp.concatenate(three_terms(pb[...]), axis=0).astype(BF16)
 
-    for target in reversed(evens):
-        @pl.when(jnp.logical_and(target != z, target < TILES))
+    for k in reversed(Z_FAR):
+        tile = tile_of(z_peer[k])
+
+        @pl.when(owns(z_peer[k]))
         def _():
-            tiles = full.at[my_rows, pl.ds(pl.multiple_of(core * HALF + target // 2 * 256, 256), 256)]
-            wait_on(owner_sem.at[target // 2], tiles)
-            for k in X_FAR:
-                remote(6, tiles, tiles, x_peer[k], recv.at[5 + k]).start()
+            done = full.at[my_rows, tile_columns(tile)]
+            wait_on(owner_sem.at[tile], done)
+            for i in X_FAR:
+                remote(6, done, done, x_peer[i], recv.at[5 + i]).start()
 
     piece = full.at[my_rows, my_half]
     remote(7, piece, piece, partner, recv.at[9]).start()
@@ -223,13 +235,12 @@
     gram = folded(dot(low[...], low[...], NT))
     cross = folded(dot(low[...], pb_low[...], NT))
     gram_all[y] = jnp.concatenate([gram, cross, jnp.zeros((R, 128 - 2 * R), F32)], axis=1)
-    for k in Y_FAR:
-        remote(9, gram_all.at[y], gram_all.at[y], at(x, z, core, y_peer[k]), recv.at[11]).start()
-
     wait_on(recv.at[10], r_y)
     z_tile = s_y[y]
     for k in range(NY - 1):
         z_tile = z_tile + r_y[k]
+    for k in Y_FAR:
+        remote(9, gram_all.at[y], gram_all.at[y], at(x, z, core, y_peer[k]), recv.at[11]).start()
 
     terms = jnp.concatenate((*three_terms(z_tile), jnp.zeros((8, 128), F32)), axis=0).astype(BF16)
     tokens = lax.rem(y, 2)
@@ -263,7 +274,7 @@
     wait_on(recv.at[16], r_qx)
     s_qz[...] = s_qx[0] + r_qx[0] + r_qx[1] + r_qx[2]
 
-    for a in Z_EVEN:
+    for a in Z_PAIR:
         target = lax.rem(z + a - lax.rem(z + core, 2), NZ)
         slot = lax.rem(z - target + NZ, NZ) - 1
 
@@ -310,7 +321,7 @@
 
     @pl.when(owner)
     def _():
-        wait_on(send.at[4], s_z.at[pl.ds(0, TILES // 2 - 1)])
+        wait_on(send.at[4], s_z.at[pl.ds(0, TILES - 1)])
         wait_on(send.at[5], r_z)
 
     @pl.when(jnp.logical_not(owner))
@@ -368,9 +379,9 @@
             vmem((R, HALF), F32),
             vmem((NX - 1, 8, 1024), F32),
             vmem((NX - 1, 8, HALF - 1024), F32),
-            vmem((TILES // 2, 8, 256), F32),
-            vmem((NZ - 1, 8, 256), F32),
-            vmem((R, 256), F32),
+            vmem((TILES, 8, 128), F32),
+            vmem((NZ - 1, 8, 128), F32),
+            vmem((R, 128), F32),
             vmem((R, FF), F32),
             vmem((3 * R, FF), BF16),
             vmem((NY, 8, 128), F32),
@@ -388,7 +399,7 @@
             dma((4 + 2 * G_CHUNKS,)),
             dma((17,)),
             dma((19,)),
-            dma((TILES // 2,)),
+            dma((TILES,)),
         ],
         compiler_params=pltpu.CompilerParams(collective_id=0, has_side_effects=True),
         name="powersgd",

time: 73 us -> 72.3 us (level)
  no operation moved by 1% of the time
where the time goes in v3:
time: 72.3 us; the launch traced here: 72.2 us
  Pallas kernels  71.6 us (99%)
    pallas_call x1, Pallas kernels, on_device(): pl.pallas_call(kernel, out_shape=(vmem((R, FF), F32), vmem((R, D // REPLI...  70.8 us

profile of v3, /device:TPU:1, one launch (start us, length us, event | category | flops | bytes accessed | tf_op | source)
XLA Modules:
  0.0 72.2 jit_solution(3595357569683494799)
XLA Ops:
  0.6 70.8 %powersgd.1 = (f32[32,3584]{1,0:T(8,128)S(1)}, f32[32,64]{1,0:T(8,128)S(1)}) custom-call(bf16[128,3584]{1,0:T(8,128)(2,1)} %hidden.1, bf16[128,8192]{1,0:T(8,128)(2,1)} %out_grad.1, bf16[128,3584]{1,0:T(8,128)(2,1)} %prev_hidden.1, bf16[128,8192]{1,0:T(8,128)(2,1)} %prev_grad.1, f32[32,3584]{1,0:T(8,128)} %bitcast.5, f32[32,8192]{1,0:T(8,128)} %bitcast.4), custom_call_target="tpu_custom_call" | custom-call | tf_op jit(solution)/shard_map/powersgd/pallas_call | solution.py:364
  71.4 0.8 %hand_over.1 = (f32[32,3584]{1,0:T(8,128)}, f32[32,64]{1,0:T(8,128)}) custom-call(f32[32,3584]{1,0:T(8,128)S(1)} %get-tuple-element.6.basis, f32[32,64]{1,0:T(8,128)S(1)} %get-tuple-element.7.factor), custom_call_target="tpu_custom_call" | custom-call | tf_op jit(solution)/shard_map/hand_over/pallas_call | solution.py:407

commit v4 on v3

--- a/solution.py
+++ b/solution.py
@@ -103,9 +103,14 @@
                 pltpu.make_async_copy(g.at[:, cols], grad.at[s, :, cols], load_sem.at[1 + 2 * j + s])
             )
     n = 1 + 2 * G_CHUNKS
-    loads.append(pltpu.make_async_copy(hidden, hid.at[pl.ds(0, TOK), :], load_sem.at[n]))
-    loads.append(pltpu.make_async_copy(prev_hidden, hid.at[pl.ds(TOK, TOK), :], load_sem.at[n + 1]))
-    loads.append(pltpu.make_async_copy(basis_t, pb, load_sem.at[n + 2]))
+    my_half = pl.ds(pl.multiple_of(core * HALF, 128), HALF)
+    other_half = pl.ds(pl.multiple_of(other * HALF, 128), HALF)
+    for i, cols in enumerate((other_half, my_half)):
+        for s, h in enumerate((hidden, prev_hidden)):
+            loads.append(
+                pltpu.make_async_copy(h.at[:, cols], hid.at[pl.ds(s * TOK, TOK), cols], load_sem.at[n + 2 * i + s])
+            )
+    loads.append(pltpu.make_async_copy(basis_t, pb, load_sem.at[n + 4]))
     for copy in loads:
         copy.start()
 
@@ -139,7 +144,6 @@
 
     loads[n].wait()
     loads[n + 1].wait()
-    my_half = pl.ds(pl.multiple_of(core * HALF, 128), HALF)
     chunks = ((0, 1024), (1024, HALF - 1024))
     for i, (start, size) in enumerate(chunks):
         there = pl.ds(pl.multiple_of(other * HALF + start, 128), size)
@@ -149,6 +153,8 @@
             pl.semaphore_wait(barrier, 1 + (NX - 1) + 2 * (NY - 1) + TILES - owner.astype(jnp.int32))
         remote(i, s_core.at[:, here], r_core.at[:, here], partner).start()
     r_x = (r_x0, r_x1)
+    loads[n + 2].wait()
+    loads[n + 3].wait()
     for i, (start, size) in enumerate(chunks):
         mine = pl.ds(pl.multiple_of(core * HALF + start, 128), size)
         here = pl.ds(start, size)
@@ -172,7 +178,7 @@
             def _():
                 remote(4, s_z.at[tile], r_z.at[NZ - 1 - k], at(x, z_peer[k], core, y)).start()
 
-    loads[n + 2].wait()
+    loads[n + 4].wait()
     my_tile = jnp.minimum(tile_of(z), TILES - 1)
 
     def tile_columns(tile):
@@ -218,7 +224,7 @@
 
     zt = pulled_half(my_half)
     wait_on(recv.at[9], r_core)
-    zt = zt + pulled_half(pl.ds(pl.multiple_of(other * HALF, 128), HALF))
+    zt = zt + pulled_half(other_half)
     zt = zt[0:R] + zt[R : 2 * R] + zt[2 * R : 3 * R]
 
     for g in range(4):
@@ -287,6 +293,8 @@
     for k in range(1, NY):
         sums = sums + gram_all[k]
     inverse = inverse_cholesky(sums)
+    i1, i2, i3 = three_terms(inverse)
+    inverse_terms = jnp.concatenate([i1, i1, i1, i2, i2, i3], axis=1).astype(BF16)
     cross_all = sums[:, R : 2 * R]
     scaled = inverse * jnp.sqrt(F32(FF_ALL))
     new_basis_t[...] = dot(scaled, full[...], NN, HIGHEST)
@@ -305,15 +313,6 @@
             for pc in (core, other):
                 remote(16, s_f, r_f.at[y], at(x, z, pc, y_peer[k]), recv.at[18]).start()
         remote(16, s_f, r_f.at[y], partner, recv.at[18]).start()
-        wait_on(recv.at[18], r_f.at[pl.ds(0, NY - 1)])
-
-    @pl.when(jnp.logical_not(keeps))
-    def _():
-        wait_on(recv.at[18], r_f)
-
-    q_t = jnp.concatenate([r_f[2 * g] + r_f[2 * g + 1] for g in range(4)], axis=0)
-    result = dot(inverse, q_t * (1.0 / REPLICAS) - taken, NN, HIGHEST)
-    new_factor_t[...] = jnp.where(core == 0, result[:, 0:64], result[:, 64:128])
 
     for i, (start, size) in enumerate(chunks):
         wait_on(send.at[i], s_core.at[:, pl.ds(start, size)])
@@ -339,11 +338,27 @@
     @pl.when(keeps)
     def _():
         wait_on(send.at[11], s_qz.at[pl.ds(0, NZ // 2 - 1)])
+
+    @pl.when(jnp.logical_not(keeps))
+    def _():
+        wait_on(send.at[11], s_qz)
+
+    @pl.when(keeps)
+    def _():
+        wait_on(recv.at[18], r_f.at[pl.ds(0, NY - 1)])
+
+    @pl.when(jnp.logical_not(keeps))
+    def _():
+        wait_on(recv.at[18], r_f)
+
+    q_t = jnp.concatenate([r_f[2 * g] + r_f[2 * g + 1] for g in range(4)], axis=0)
+    q1, q2, q3 = three_terms(q_t * (1.0 / REPLICAS) - taken)
+    result = dot(inverse_terms, jnp.concatenate([q1, q2, q3, q1, q2, q1], axis=0).astype(BF16), NN)
+    new_factor_t[...] = jnp.where(core == 0, result[:, 0:64], result[:, 64:128])
+
+    @pl.when(keeps)
+    def _():
         wait_on(send.at[16], r_qz)
-
-    @pl.when(jnp.logical_not(keeps))
-    def _():
-        wait_on(send.at[11], s_qz)
 
 
 def hand_over(basis, factor, new_basis_t, new_factor_t, sem):
@@ -396,7 +411,7 @@
             vmem((NZ - 1, 8, 128), F32),
             vmem((8, 128), F32),
             vmem((NY, 8, 128), F32),
-            dma((4 + 2 * G_CHUNKS,)),
+            dma((6 + 2 * G_CHUNKS,)),
             dma((17,)),
             dma((19,)),
             dma((TILES,)),

time: 72.3 us -> 72.2 us (level)
  no operation moved by 1% of the time
where the time goes in v4:
time: 72.2 us; the launch traced here: 72.1 us
  Pallas kernels  71.4 us (99%)
    pallas_call x1, Pallas kernels, on_device(): pl.pallas_call(kernel, out_shape=(vmem((R, FF), F32), vmem((R, D // REPLI...  70.6 us

profile of v4, /device:TPU:1, one launch (start us, length us, event | category | flops | bytes accessed | tf_op | source)
XLA Modules:
  0.0 72.1 jit_solution(16737896593328231995)
XLA Ops:
  0.6 70.6 %powersgd.1 = (f32[32,3584]{1,0:T(8,128)S(1)}, f32[32,64]{1,0:T(8,128)S(1)}) custom-call(bf16[128,3584]{1,0:T(8,128)(2,1)} %hidden.1, bf16[128,8192]{1,0:T(8,128)(2,1)} %out_grad.1, bf16[128,3584]{1,0:T(8,128)(2,1)} %prev_hidden.1, bf16[128,8192]{1,0:T(8,128)(2,1)} %prev_grad.1, f32[32,3584]{1,0:T(8,128)} %bitcast.5, f32[32,8192]{1,0:T(8,128)} %bitcast.4), custom_call_target="tpu_custom_call" | custom-call | tf_op jit(solution)/shard_map/powersgd/pallas_call | solution.py:379
  71.3 0.8 %hand_over.1 = (f32[32,3584]{1,0:T(8,128)}, f32[32,64]{1,0:T(8,128)}) custom-call(f32[32,3584]{1,0:T(8,128)S(1)} %get-tuple-element.6.basis, f32[32,64]{1,0:T(8,128)S(1)} %get-tuple-element.7.factor), custom_call_target="tpu_custom_call" | custom-call | tf_op jit(solution)/shard_map/hand_over/pallas_call | solution.py:422
